TPU v7x, 256 devices: a whole 4x4x8 slice. The times are simulated.
256 devices in a mesh: row: 16 (over x_lo, y, core), col: 16 (over x_hi, z).
Axes of the slice: x: 4 (x_hi: 2, x_lo: 2; x = x_hi * 2 + x_lo), y: 4, z: 8, core: 2. Of those that a mesh axis runs over, the one named last changes fastest.
Arguments:
- node_features: bfloat16 [65536, 256], P(('row', 'col')), may hold values from -6 to 6
- tile_values: bfloat16 [16, 16, 128, 128, 128], P('row', 'col'), may hold values from -0.09375 to 0.09375
- tile_coords: int32 [16, 16, 128, 2], P('row', 'col'), may hold values from 0 to 31, as said below
- tile_counts: int32 [16, 16], P('row', 'col'), may hold values from 32 to 128, as said below
- first_weight: bfloat16 [256, 256], replicated, may hold values from -0.375 to 0.375
- second_weight: bfloat16 [256, 128], replicated, may hold values from -0.375 to 0.375
- out_grad: bfloat16 [65536, 128], P(('row', 'col')), may hold values from -6 to 6
Outputs:
- output: bfloat16 [65536, 128], P(('row', 'col'))
- first_grad: float32 [256, 256], replicated
- second_grad: float32 [256, 128], replicated
Inputs may be any that keep to these rules, and one draw needn't show every extreme that they name: `tile_counts`: each grid cell uses at least 32 slots; at least one grid cell uses all 128 in every draw. `tile_coords`: the first entry is a tile row below 32, the second a tile column below 32; within one grid cell no two slots share a position.
All inputs are finite; a program needn't handle non-finite values.
Results may differ from a plain program's by a relative error of at most 0.005.
Values may be sent and summed in bfloat16 or wider, within the bound.
A program may use at most 64 MiB of HBM per device.

v0:
```python
import math
import jax
import jax.numpy as jnp
from jax import lax
from jax.sharding import PartitionSpec as P

HIGHEST = lax.Precision.HIGHEST


def tile_sum(tile_block, dest_index, source_index, live_slots, source, dest_tiles, flipped):
    slot_count = tile_block.shape[0]
    group_size = math.gcd(slot_count, 32)
    round_count = slot_count // group_size
    edge_size = tile_block.shape[1]
    width_size = source.shape[-1]
    grouped_tiles = tile_block.reshape(round_count, group_size, edge_size, edge_size)
    grouped_dest = dest_index.reshape(round_count, group_size)
    grouped_source = source_index.reshape(round_count, group_size)
    grouped_live = live_slots.reshape(round_count, group_size)
    target_ids = jnp.arange(dest_tiles, dtype=jnp.int32)
    einsum_form = "tba,tbw->taw" if flipped else "tab,tbw->taw"

    def add_group(running, pieces):
        group_tiles, group_dest, group_source, group_live = pieces
        picked = jnp.take(source, group_source, axis=0)
        products = jnp.einsum(einsum_form, group_tiles, picked, preferred_element_type=jnp.float32)
        select = ((group_dest[:, None] == target_ids[None, :]) & group_live[:, None]).astype(
            jnp.float32
        )
        running = running + jnp.einsum("tr,taw->raw", select, products, precision=HIGHEST)
        return (running, None)

    start_sum = jnp.zeros((dest_tiles, edge_size, width_size), jnp.float32)
    running, unused = lax.scan(
        add_group, start_sum, (grouped_tiles, grouped_dest, grouped_source, grouped_live)
    )
    return running.reshape(dest_tiles * edge_size, width_size)


def on_device(
    node_features, tile_values, tile_coords, tile_counts, first_weight, second_weight, out_grad
):
    node_rows = node_features.shape[0]
    edge_size = tile_values.shape[-1]
    slot_count = tile_values.shape[2]
    grid_rows = lax.axis_size("row")
    grid_cols = lax.axis_size("col")
    row_tiles = grid_rows * node_rows // edge_size
    col_tiles = grid_cols * node_rows // edge_size
    tile_block = tile_values.reshape(slot_count, edge_size, edge_size)
    flat_coords = tile_coords.reshape(slot_count, 2)
    tile_row = flat_coords[:, 0]
    tile_col = flat_coords[:, 1]
    live_slots = jnp.arange(slot_count, dtype=jnp.int32) < tile_counts.reshape(())
    gathered_x = lax.all_gather(node_features, "col", axis=0, tiled=True)
    feature_part = tile_sum(
        tile_block,
        tile_row,
        tile_col,
        live_slots,
        gathered_x.reshape(col_tiles, edge_size, -1),
        row_tiles,
        False,
    )
    first_mean = lax.psum_scatter(feature_part, "row", scatter_dimension=0, tiled=True)
    first_pre = jnp.dot(first_mean, first_weight.astype(jnp.float32), precision=HIGHEST)
    hidden_act = jax.nn.silu(first_pre).astype(jnp.bfloat16)
    second_wide = second_weight.astype(jnp.float32)
    gathered_h = lax.all_gather(hidden_act, "col", axis=0, tiled=True)
    hidden_part = tile_sum(
        tile_block,
        tile_row,
        tile_col,
        live_slots,
        gathered_h.reshape(col_tiles, edge_size, -1),
        row_tiles,
        False,
    )
    second_mean = lax.psum_scatter(hidden_part, "row", scatter_dimension=0, tiled=True)
    logit_rows = jnp.dot(second_mean, second_wide, precision=HIGHEST)
    output = logit_rows.astype(jnp.bfloat16)
    gathered_g = lax.all_gather(out_grad, "row", axis=0, tiled=True)
    grad_part = tile_sum(
        tile_block,
        tile_col,
        tile_row,
        live_slots,
        gathered_g.reshape(row_tiles, edge_size, -1),
        col_tiles,
        True,
    )
    back_sum = lax.psum_scatter(grad_part, "col", scatter_dimension=0, tiled=True)
    scale = 1.0 / math.sqrt(node_rows * grid_rows * grid_cols)
    second_local = jnp.dot(hidden_act.astype(jnp.float32).T, back_sum, precision=HIGHEST) * scale
    hidden_grad = jnp.dot(back_sum, second_wide.T, precision=HIGHEST)
    sigma = jax.nn.sigmoid(first_pre)
    pre_grad = hidden_grad * (sigma * (1.0 + first_pre * (1.0 - sigma)))
    second_grad = lax.psum(second_local, ("row", "col"))
    first_local = jnp.dot(first_mean.T, pre_grad, precision=HIGHEST) * scale
    first_grad = lax.psum(first_local, ("row", "col"))
    return (output, first_grad, second_grad)


def solution(mesh):
    return jax.shard_map(
        on_device,
        mesh=mesh,
        in_specs=(
            P(("row", "col"), None),
            P("row", "col", None, None, None),
            P("row", "col", None, None),
            P("row", "col"),
            P(),
            P(),
            P(("row", "col"), None),
        ),
        out_specs=(P(("row", "col"), None), P(), P()),
        check_vma=False,
    )
```

profile of v0, /device:TPU:1, one launch (start us, length us, event | category | flops | bytes accessed | tf_op | source)
XLA Modules:
  0.0 898.8 jit_solution(9143985936863349914)
XLA Ops:
  9.6 86.8 %all-gather.4.cloned.1.call-done = bf16[4096,256]{1,0:T(8,128)(2,1)} async-done(((bf16[256,256]{1,0:T(8,128)(2,1)}), bf16[4096,256]{1,0:T(8,128)(2,1)}) %all-gather.4.cloned.1.call-update) | async-done | bytes 2097168 | tf_op jit(solution)/shard_map/all_gather | solution.py:55
  96.3 64.7 %while.33 = (s32[]{:T(128)}, f32[32,128,256]{2,0,1:T(8,128)}, s32[4,32]{1,0:T(4,128)S(1)}, pred[4,32]{1,0:T(4,128)(4,1)S(1)}, bf16[4,32,128,128]{3,2,1,0:T(8,128...) while((s32[]{:T(128)}, f32[32,128,256]{2,0,1:T(8,128)}, ...), condition=%wide.region_1.3_spmd.clone, body=%wide.region_0.2_spmd.clone.sunk | while | flops 674237632 | bytes 24123028 | solution.py:34
  98.6 4.0 fusion.96
  102.6 8.9 select_add_fusion.6
  113.9 4.0 fusion.96
  117.9 10.2 %select_add_fusion.6 = f32[32,128,256]{2,0,1:T(8,128)} fusion(f32[32,128,256]{2,0,1:T(8,128)} %get-tuple-element.410, f32[32,128,256]{2,1,0:T(8,128)} %fusion.96, pred[]{:T(512)S(6)} %compare.9, s32[32]{0:T(128)S(1)} %fusion.97, pred[32]{0:T(512)(128)(4,1)S(1)} %dynamic-slice_bitcast_fusion.6), kind=kOutput, calls=%fused_computation.33.clone.1 | convolution fusion | flops 404752384 | bytes 12583073 | tf_op jit(solution)/shard_map/while/body/eval_jaxpr/tr,taw->raw/dot_general | solution.py:30
  130.4 4.0 fusion.96
  134.4 10.2 %select_add_fusion.6 = f32[32,128,256]{2,0,1:T(8,128)} fusion(f32[32,128,256]{2,0,1:T(8,128)} %get-tuple-element.410, f32[32,128,256]{2,1,0:T(8,128)} %fusion.96, pred[]{:T(512)S(6)} %compare.9, s32[32]{0:T(128)S(1)} %fusion.97, pred[32]{0:T(512)(128)(4,1)S(1)} %dynamic-slice_bitcast_fusion.6), kind=kOutput, calls=%fused_computation.33.clone.1 | convolution fusion | flops 404752384 | bytes 12583073 | tf_op jit(solution)/shard_map/while/body/eval_jaxpr/tr,taw->raw/dot_general | solution.py:30
  146.9 4.0 fusion.96
  150.9 10.2 %select_add_fusion.6 = f32[32,128,256]{2,0,1:T(8,128)} fusion(f32[32,128,256]{2,0,1:T(8,128)} %get-tuple-element.410, f32[32,128,256]{2,1,0:T(8,128)} %fusion.96, pred[]{:T(512)S(6)} %compare.9, s32[32]{0:T(128)S(1)} %fusion.97, pred[32]{0:T(512)(128)(4,1)S(1)} %dynamic-slice_bitcast_fusion.6), kind=kOutput, calls=%fused_computation.33.clone.1 | convolution fusion | flops 404752384 | bytes 12583073 | tf_op jit(solution)/shard_map/while/body/eval_jaxpr/tr,taw->raw/dot_general | solution.py:30
  161.0 6.6 copy.10
  168.5 65.5 %reduce-scatter.4.cloned.1.call-done = f32[256,256]{1,0:T(8,128)} async-done(((f32[4096,256]{1,0:T(8,128)}), f32[256,256]{1,0:T(8,128)}) %reduce-scatter.4.cloned.1.call-update) | async-done | bytes 262160 | tf_op jit(solution)/shard_map/reduce_scatter | solution.py:65
  236.2 37.0 %all-gather.8.cloned.1.call-done = bf16[4096,128]{1,0:T(8,128)(2,1)} async-done(((bf16[256,128]{1,0:T(8,128)(2,1)}), bf16[4096,128]{1,0:T(8,128)(2,1)}) %all-gather.8.cloned.1.call-update) | async-done | bytes 1048592 | tf_op jit(solution)/shard_map/all_gather | solution.py:82
  273.2 35.7 %while.35 = (s32[]{:T(128)}, f32[32,128,128]{2,0,1:T(8,128)}, s32[4,32]{1,0:T(4,128)S(1)}, pred[4,32]{1,0:T(4,128)(4,1)S(1)}, bf16[4,32,128,128]{3,2,1,0:T(8,128...) while((s32[]{:T(128)}, f32[32,128,128]{2,0,1:T(8,128)}, ...), condition=%wide.region_7.9_spmd.clone, body=%wide.region_6.8_spmd.clone.sunk | while | flops 337120544 | bytes 12588823 | solution.py:34
  284.7 5.4 select_add_fusion.8
  294.0 5.5 select_add_fusion.8
  303.4 5.5 select_add_fusion.8
  308.8 4.2 copy.12
  313.0 44.8 %all-gather.6.cloned.1.call-done = bf16[4096,256]{1,0:T(8,128)(2,1)} async-done(((bf16[256,256]{1,0:T(8,128)(2,1)}), bf16[4096,256]{1,0:T(8,128)(2,1)}) %all-gather.6.cloned.1.call-update) | async-done | bytes 2097168 | tf_op jit(solution)/shard_map/all_gather | solution.py:69
  357.8 65.0 %while.34 = (s32[]{:T(128)}, f32[32,128,256]{2,0,1:T(8,128)}, s32[4,32]{1,0:T(4,128)S(1)}, pred[4,32]{1,0:T(4,128)(4,1)S(1)}, bf16[4,32,128,128]{3,2,1,0:T(8,128...) while((s32[]{:T(128)}, f32[32,128,256]{2,0,1:T(8,128)}, ...), condition=%wide.region_4.6_spmd.clone, body=%wide.region_3.5_spmd.clone.sunk | while | flops 674237632 | bytes 24123028 | solution.py:34
  360.1 4.0 fusion.102
  364.1 8.9 select_add_fusion.7
  375.4 4.0 fusion.102
  379.4 10.2 %select_add_fusion.7 = f32[32,128,256]{2,0,1:T(8,128)} fusion(f32[32,128,256]{2,0,1:T(8,128)} %get-tuple-element.437, f32[32,128,256]{2,1,0:T(8,128)} %fusion.102, pred[]{:T(512)S(6)} %compare.10, s32[32]{0:T(128)S(1)} %fusion.103, pred[32]{0:T(512)(128)(4,1)S(1)} %dynamic-slice_bitcast_fusion.7), kind=kOutput, calls=%fused_computation.57.clone.1 | convolution fusion | flops 404752384 | bytes 12583073 | tf_op jit(solution)/shard_map/while/body/eval_jaxpr/tr,taw->raw/dot_general | solution.py:30
  392.0 4.0 fusion.102
  396.0 10.3 %select_add_fusion.7 = f32[32,128,256]{2,0,1:T(8,128)} fusion(f32[32,128,256]{2,0,1:T(8,128)} %get-tuple-element.437, f32[32,128,256]{2,1,0:T(8,128)} %fusion.102, pred[]{:T(512)S(6)} %compare.10, s32[32]{0:T(128)S(1)} %fusion.103, pred[32]{0:T(512)(128)(4,1)S(1)} %dynamic-slice_bitcast_fusion.7), kind=kOutput, calls=%fused_computation.57.clone.1 | convolution fusion | flops 404752384 | bytes 12583073 | tf_op jit(solution)/shard_map/while/body/eval_jaxpr/tr,taw->raw/dot_general | solution.py:30
  408.6 4.0 fusion.102
  412.6 10.2 %select_add_fusion.7 = f32[32,128,256]{2,0,1:T(8,128)} fusion(f32[32,128,256]{2,0,1:T(8,128)} %get-tuple-element.437, f32[32,128,256]{2,1,0:T(8,128)} %fusion.102, pred[]{:T(512)S(6)} %compare.10, s32[32]{0:T(128)S(1)} %fusion.103, pred[32]{0:T(512)(128)(4,1)S(1)} %dynamic-slice_bitcast_fusion.7), kind=kOutput, calls=%fused_computation.57.clone.1 | convolution fusion | flops 404752384 | bytes 12583073 | tf_op jit(solution)/shard_map/while/body/eval_jaxpr/tr,taw->raw/dot_general | solution.py:30
  422.8 6.6 copy.11
  429.5 131.3 %reduce-scatter.8.cloned.1.call-done = f32[256,128]{1,0:T(8,128)} async-done(((f32[4096,128]{1,0:T(8,128)}), f32[256,128]{1,0:T(8,128)}) %reduce-scatter.8.cloned.1.call-update) | async-done | bytes 131088 | tf_op jit(solution)/shard_map/reduce_scatter | solution.py:92
  565.2 67.1 %reduce-scatter.6.cloned.1.call-done = f32[256,256]{1,0:T(8,128)} async-done(((f32[4096,256]{1,0:T(8,128)}), f32[256,256]{1,0:T(8,128)}) %reduce-scatter.6.cloned.1.call-update) | async-done | bytes 262160 | tf_op jit(solution)/shard_map/reduce_scatter | solution.py:79
  634.2 254.5 %all-reduce.3.cloned.1.call-done = (f32[256,256]{1,0:T(8,128)}, f32[256,128]{1,0:T(8,128)}) async-done(((f32[256,256]{1,0:T(8,128)}, f32[256,128]{1,0:T(8,128)}), (f32[256,256]{1,0:T(8,128)}, f32[256,128]{1,0:T(8,128)})) %all-reduce.3.cloned.1.call-update) | async-done | bytes 393232 | tf_op jit(solution)/shard_map/psum | solution.py:100
  (105 shorter events, 51.9 us)
Async XLA Ops:
  7.2 226.8 %copy-start = (bf16[256,256]{1,0:T(8,128)(2,1)S(1)}, bf16[256,256]{1,0:T(8,128)(2,1)}, u32[]{:S(2)}) copy-start(bf16[256,256]{1,0:T(8,128)(2,1)} %param.19) | copy-start | bytes 393220
  7.2 89.2 %all-gather.4.cloned.1.call-start = ((), (), s32[]{:S(2)}) async-start(), calls=%async_computation.3 | async-start | bytes 2228224 | tf_op jit(solution)/shard_map/all_gather | solution.py:55
  7.9 226.1 %reduce-scatter.4.cloned.1.call-start = ((), (), s32[]{:S(2)}) async-start(), calls=%async_computation.4 | async-start | bytes 4456448 | tf_op jit(solution)/shard_map/reduce_scatter | solution.py:65
  167.7 105.5 %all-gather.8.cloned.1.call-start = ((), (), s32[]{:S(2)}) async-start(), calls=%async_computation.7 | async-start | bytes 1114112 | tf_op jit(solution)/shard_map/all_gather | solution.py:82
  168.4 189.4 %all-gather.6.cloned.1.call-start = ((), (), s32[]{:S(2)}) async-start(), calls=%async_computation.5 | async-start | bytes 2228224 | tf_op jit(solution)/shard_map/all_gather | solution.py:69
  235.9 324.9 %reduce-scatter.8.cloned.1.call-start = ((), (), s32[]{:S(2)}) async-start(), calls=%async_computation.8 | async-start | bytes 2228224 | tf_op jit(solution)/shard_map/reduce_scatter | solution.py:92
  313.0 319.3 %reduce-scatter.6.cloned.1.call-start = ((), (), s32[]{:S(2)}) async-start(), calls=%async_computation.6 | async-start | bytes 4456448 | tf_op jit(solution)/shard_map/reduce_scatter | solution.py:79
  429.4 131.4 %copy-start.1 = (bf16[256,256]{1,0:T(8,128)(2,1)S(1)}, bf16[256,256]{1,0:T(8,128)(2,1)}, u32[]{:S(2)}) copy-start(bf16[256,256]{1,0:T(8,128)(2,1)} %get-tuple-element.261) | copy-start | bytes 393220
  429.4 133.3 %copy-start.3 = (bf16[256,128]{1,0:T(8,128)(2,1)S(1)}, bf16[256,128]{1,0:T(8,128)(2,1)}, u32[]{:S(2)}) copy-start(bf16[256,128]{1,0:T(8,128)(2,1)} %param.20) | copy-start | bytes 196612
  429.4 134.5 %copy-start.2 = (f32[256,256]{1,0:T(8,128)S(1)}, f32[256,256]{1,0:T(8,128)}, u32[]{:S(2)}) copy-start(f32[256,256]{1,0:T(8,128)} %reduce-scatter.4.cloned.1.call-done) | copy-start | bytes 786436
  429.4 459.3 %all-reduce.3.cloned.1.call-start = ((), (), s32[]{:S(2)}) async-start(), calls=%async_computation.9 | async-start | bytes 786432 | tf_op jit(solution)/shard_map/psum | solution.py:100
Sparse Core Ops, SparseCore 0:
  10.6 85.6 all-gather.3
  167.8 66.1 reduce-scatter.3
  235.9 37.2 all-gather.7
  276.2 81.5 all-gather.5
  361.5 199.2 reduce-scatter.7
  563.2 69.0 reduce-scatter.5
  638.4 250.2 all-reduce.2
where the time goes:
time: 900 us; the launch traced here: 899 us
  waiting for transfers between devices  688 us (76%)
  matrix products  147 us (16%)
  local copies, waits for them, and re-layouts  47.9 us (5%)
  between operations  14.8 us (2%)
    psum x1, waiting for transfers between devices, on_device(): first_grad = lax.psum(first_local, ('row', 'col'))  255 us
    reduce_scatter x1, waiting for transfers between devices, on_device(): lax.psum_scatter(grad_part, 'col', scatter_dimension=0, tiled=True)  131 us
    dot_general x12, matrix products, add_group(): jnp.einsum('tr,taw->raw', select, products, precision=HIGHEST)  99.3 us
    all_gather x1, waiting for transfers between devices, on_device(): gathered_x = lax.all_gather(node_features, 'col', axis=0, tiled=True)  86.8 us
    reduce_scatter x1, waiting for transfers between devices, on_device(): lax.psum_scatter(hidden_part, 'row', scatter_dimension=0, tiled=True)  67.1 us
    reduce_scatter x1, waiting for transfers between devices, on_device(): lax.psum_scatter(feature_part, 'row', scatter_dimension=0, tiled=True)  65.5 us
    all_gather x1, waiting for transfers between devices, on_device(): gathered_h = lax.all_gather(hidden_act, 'col', axis=0, tiled=True)  44.8 us
    dot_general x12, matrix products, add_group(): jnp.einsum(einsum_form, group_tiles, picked, preferred_element_type=jnp.f...  39.1 us
  transfers between devices with their start and end apart: 7, of which 7 were waited for; matrix products, arithmetic and copies ran while one was open for 13% of the time, Pallas kernels for 0%

commit v1 on v0

--- a/solution.py
+++ b/solution.py
@@ -97,7 +97,8 @@
     pre_grad = hidden_grad * (sigma * (1.0 + first_pre * (1.0 - sigma)))
     second_grad = lax.psum(second_local, ("row", "col"))
     first_local = jnp.dot(first_mean.T, pre_grad, precision=HIGHEST) * scale
-    first_grad = lax.psum(first_local, ("row", "col"))
+    half = lax.psum(first_local, "row")
+    first_grad = lax.psum(half, "col")
     return (output, first_grad, second_grad)
 
 

time: 900 us -> 1140 us (1.27); the launches traced: 899 us -> 1130 us
  waiting for transfers between devices: 688 us -> 916 us
    psum x1 -> x3, waiting for transfers between devices: 255 us -> 446 us  [the longest x1 248 us: on_device(): second_grad = lax.psum(second_local, ('row', 'col'))]
    reduce_scatter x1, waiting for transfers between devices: 131 us -> 203 us  [on_device(): lax.psum_scatter(grad_part, 'col', scatter_dimension=0, tiled=True)]
    reduce_scatter x1, waiting for transfers between devices: 65.5 us -> 25.9 us  [on_device(): lax.psum_scatter(feature_part, 'row', scatter_dimension=0, tiled=True)]
    all_gather x1, waiting for transfers between devices: 44.8 us -> 84.3 us  [on_device(): gathered_h = lax.all_gather(hidden_act, 'col', axis=0, tiled=True)]
    all_gather x1, waiting for transfers between devices: 37 us -> 0.02 us  [on_device(): gathered_g = lax.all_gather(out_grad, 'row', axis=0, tiled=True)]
  transfers between devices with their start and end apart: 7 -> 9, of which waited for: 7 -> 8; matrix products, arithmetic and copies ran while one was open for 13% -> 17% of each run, Pallas kernels for 0% -> 0%
where the time goes in v1:
time: 1140 us; the launch traced here: 1130 us
  waiting for transfers between devices  916 us (80%)
  matrix products  146 us (13%)
  local copies, waits for them, and re-layouts  48.7 us (4%)
  between operations  14.6 us (1%)
    psum x1, waiting for transfers between devices, on_device(): second_grad = lax.psum(second_local, ('row', 'col'))  248 us
    reduce_scatter x1, waiting for transfers between devices, on_device(): lax.psum_scatter(grad_part, 'col', scatter_dimension=0, tiled=True)  203 us
    psum x1, waiting for transfers between devices, on_device(): first_grad = lax.psum(half, 'col')  146 us
    dot_general x12, matrix products, add_group(): jnp.einsum('tr,taw->raw', select, products, precision=HIGHEST)  99.2 us
    all_gather x1, waiting for transfers between devices, on_device(): gathered_x = lax.all_gather(node_features, 'col', axis=0, tiled=True)  86 us
    all_gather x1, waiting for transfers between devices, on_device(): gathered_h = lax.all_gather(hidden_act, 'col', axis=0, tiled=True)  84.3 us
    reduce_scatter x1, waiting for transfers between devices, on_device(): lax.psum_scatter(hidden_part, 'row', scatter_dimension=0, tiled=True)  69.6 us
    psum x1, waiting for transfers between devices, on_device(): half = lax.psum(first_local, 'row')  51.6 us
  transfers between devices with their start and end apart: 9, of which 8 were waited for; matrix products, arithmetic and copies ran while one was open for 17% of the time, Pallas kernels for 0%

profile of v1, /device:TPU:1, one launch (start us, length us, event | category | flops | bytes accessed | tf_op | source)
XLA Modules:
  0.0 1126.9 jit_solution(5448938369335001512)
XLA Ops:
  10.3 86.0 %all-gather.4.cloned.1.call-done = bf16[4096,256]{1,0:T(8,128)(2,1)} async-done(((bf16[256,256]{1,0:T(8,128)(2,1)}), bf16[4096,256]{1,0:T(8,128)(2,1)}) %all-gather.4.cloned.1.call-update) | async-done | bytes 2097168 | tf_op jit(solution)/shard_map/all_gather | solution.py:55
  96.3 64.6 %while.33 = (s32[]{:T(128)}, f32[32,128,256]{2,0,1:T(8,128)}, s32[4,32]{1,0:T(4,128)S(1)}, pred[4,32]{1,0:T(4,128)(4,1)S(1)}, bf16[4,32,128,128]{3,2,1,0:T(8,128...) while((s32[]{:T(128)}, f32[32,128,256]{2,0,1:T(8,128)}, ...), condition=%wide.region_1.3_spmd.clone, body=%wide.region_0.2_spmd.clone.sunk | while | flops 674237632 | bytes 24123028 | solution.py:34
  102.6 8.9 select_add_fusion.6
  113.8 4.0 fusion.96
  117.8 10.2 select_add_fusion.6
  130.3 4.0 fusion.96
  134.3 10.2 select_add_fusion.6
  146.8 4.0 fusion.96
  150.8 10.2 select_add_fusion.6
  161.0 6.6 copy.10
  167.8 35.7 %while.35 = (s32[]{:T(128)}, f32[32,128,128]{2,0,1:T(8,128)}, s32[4,32]{1,0:T(4,128)S(1)}, pred[4,32]{1,0:T(4,128)(4,1)S(1)}, bf16[4,32,128,128]{3,2,1,0:T(8,128...) while((s32[]{:T(128)}, f32[32,128,128]{2,0,1:T(8,128)}, ...), condition=%wide.region_7.9_spmd.clone, body=%wide.region_6.8_spmd.clone.sunk | while | flops 337120544 | bytes 12588823 | solution.py:34
  179.4 5.5 select_add_fusion.8
  188.8 5.5 select_add_fusion.8
  198.1 5.4 select_add_fusion.8
  203.6 4.2 copy.12
  207.8 25.9 %reduce-scatter.4.cloned.1.call-done = f32[256,256]{1,0:T(8,128)} async-done(((f32[4096,256]{1,0:T(8,128)}), f32[256,256]{1,0:T(8,128)}) %reduce-scatter.4.cloned.1.call-update) | async-done | bytes 262160 | tf_op jit(solution)/shard_map/reduce_scatter | solution.py:65
  235.8 202.9 %reduce-scatter.8.cloned.1.call-done = f32[256,128]{1,0:T(8,128)} async-done(((f32[4096,128]{1,0:T(8,128)}), f32[256,128]{1,0:T(8,128)}) %reduce-scatter.8.cloned.1.call-update) | async-done | bytes 131088 | tf_op jit(solution)/shard_map/reduce_scatter | solution.py:92
  442.4 84.3 %all-gather.6.cloned.1.call-done = bf16[4096,256]{1,0:T(8,128)(2,1)} async-done(((bf16[256,256]{1,0:T(8,128)(2,1)}), bf16[4096,256]{1,0:T(8,128)(2,1)}) %all-gather.6.cloned.1.call-update) | async-done | bytes 2097168 | tf_op jit(solution)/shard_map/all_gather | solution.py:69
  526.7 64.7 %while.34 = (s32[]{:T(128)}, f32[32,128,256]{2,0,1:T(8,128)}, s32[4,32]{1,0:T(4,128)S(1)}, pred[4,32]{1,0:T(4,128)(4,1)S(1)}, bf16[4,32,128,128]{3,2,1,0:T(8,128...) while((s32[]{:T(128)}, f32[32,128,256]{2,0,1:T(8,128)}, ...), condition=%wide.region_4.6_spmd.clone, body=%wide.region_3.5_spmd.clone.sunk | while | flops 674237632 | bytes 24123028 | solution.py:34
  529.0 4.0 fusion.102
  533.0 8.9 select_add_fusion.7
  544.2 4.0 fusion.102
  548.2 10.2 select_add_fusion.7
  560.7 4.0 fusion.102
  564.7 10.2 select_add_fusion.7
  577.2 4.0 fusion.102
  581.2 10.2 select_add_fusion.7
  591.4 6.6 copy.11
  600.0 51.6 %all-reduce.4.cloned.1.call-done = f32[256,256]{1,0:T(8,128)} async-done(((f32[256,256]{1,0:T(8,128)}), f32[256,256]{1,0:T(8,128)}) %all-reduce.4.cloned.1.call-update) | async-done | bytes 262160 | tf_op jit(solution)/shard_map/psum | solution.py:100
  651.7 69.6 %reduce-scatter.6.cloned.1.call-done = f32[256,256]{1,0:T(8,128)} async-done(((f32[4096,256]{1,0:T(8,128)}), f32[256,256]{1,0:T(8,128)}) %reduce-scatter.6.cloned.1.call-update) | async-done | bytes 262160 | tf_op jit(solution)/shard_map/reduce_scatter | solution.py:79
  723.1 248.1 %all-reduce.8.cloned.1.call-done = f32[256,128]{1,0:T(8,128)} async-done(((f32[256,128]{1,0:T(8,128)}), f32[256,128]{1,0:T(8,128)}) %all-reduce.8.cloned.1.call-update) | async-done | bytes 131088 | tf_op jit(solution)/shard_map/psum | solution.py:98
  971.2 145.9 %all-reduce.6.cloned.1.call-done = f32[256,256]{1,0:T(8,128)} async-done(((f32[256,256]{1,0:T(8,128)}), f32[256,256]{1,0:T(8,128)}) %all-reduce.6.cloned.1.call-update) | async-done | bytes 262160 | tf_op jit(solution)/shard_map/psum | solution.py:101
  (111 shorter events, 57.1 us)
Async XLA Ops:
  7.2 226.6 %copy-start = (bf16[256,256]{1,0:T(8,128)(2,1)S(1)}, bf16[256,256]{1,0:T(8,128)(2,1)}, u32[]{:S(2)}) copy-start(bf16[256,256]{1,0:T(8,128)(2,1)} %param.19) | copy-start | bytes 393220
  7.2 89.2 %all-gather.4.cloned.1.call-start = ((), (), s32[]{:S(2)}) async-start(), calls=%async_computation.3 | async-start | bytes 2228224 | tf_op jit(solution)/shard_map/all_gather | solution.py:55
  7.9 159.9 %all-gather.8.cloned.1.call-start = ((), (), s32[]{:S(2)}) async-start(), calls=%async_computation.7 | async-start | bytes 1114112 | tf_op jit(solution)/shard_map/all_gather | solution.py:82
  8.7 225.1 %reduce-scatter.4.cloned.1.call-start = ((), (), s32[]{:S(2)}) async-start(), calls=%async_computation.4 | async-start | bytes 4456448 | tf_op jit(solution)/shard_map/reduce_scatter | solution.py:65
  167.6 271.1 %reduce-scatter.8.cloned.1.call-start = ((), (), s32[]{:S(2)}) async-start(), calls=%async_computation.8 | async-start | bytes 2228224 | tf_op jit(solution)/shard_map/reduce_scatter | solution.py:92
  203.6 235.1 %copy-start.3 = (bf16[256,128]{1,0:T(8,128)(2,1)S(1)}, bf16[256,128]{1,0:T(8,128)(2,1)}, u32[]{:S(2)}) copy-start(bf16[256,128]{1,0:T(8,128)(2,1)} %param.20) | copy-start | bytes 196612
  207.8 318.9 %all-gather.6.cloned.1.call-start = ((), (), s32[]{:S(2)}) async-start(), calls=%async_computation.5 | async-start | bytes 2228224 | tf_op jit(solution)/shard_map/all_gather | solution.py:69
  235.7 415.9 %all-reduce.4.cloned.1.call-start = ((), (), s32[]{:S(2)}) async-start(), calls=%async_computation.9 | async-start | bytes 524288 | tf_op jit(solution)/shard_map/psum | solution.py:100
  442.1 279.1 %reduce-scatter.6.cloned.1.call-start = ((), (), s32[]{:S(2)}) async-start(), calls=%async_computation.6 | async-start | bytes 4456448 | tf_op jit(solution)/shard_map/reduce_scatter | solution.py:79
  598.0 0.9 copy-start.1
  598.0 1.0 copy-start.2
  598.0 373.2 %all-reduce.8.cloned.1.call-start = ((), (), s32[]{:S(2)}) async-start(), calls=%async_computation.11 | async-start | bytes 262144 | tf_op jit(solution)/shard_map/psum | solution.py:98
  600.0 517.2 %all-reduce.6.cloned.1.call-start = ((), (), s32[]{:S(2)}) async-start(), calls=%async_computation.10 | async-start | bytes 524288 | tf_op jit(solution)/shard_map/psum | solution.py:101
Sparse Core Ops, SparseCore 0:
  10.6 85.6 all-gather.3
  98.2 35.5 all-gather.7
  167.7 66.0 reduce-scatter.3
  237.5 201.1 reduce-scatter.7
  441.7 85.0 all-gather.5
  529.8 121.8 all-reduce.3
  654.3 66.8 reduce-scatter.5
  728.2 242.8 all-reduce.7
  974.0 143.0 all-reduce.5
